TPU v7x, 32 devices: a whole 2x2x4 slice. The times are simulated.
32 devices in a mesh: tm: 8 (over y, x, core), tile: 4 (over z).
Axes of the slice: x: 2, y: 2, z: 4, core: 2. Of those that a mesh axis runs over, the one named last changes fastest.
Arguments:
- local_inv: bfloat16 [16, 2048, 2048], P('tm', None, 'tile'), as said below
- seed_inv: float32 [8, 2048, 2048], P('tm', None, 'tile'), as said below
- band: float32 [16, 16, 3, 128, 128], P('tm', 'tile'), may hold values from -0.25 to 0.25
- pattern: int32 [16, 16, 3], P('tm', 'tile'), may hold values from 0 to 1, as said below
Outputs:
- sigma_first: float32 [8, 2048, 2048], P('tm', None, 'tile')
- variances: float32 [16, 2048], P('tm', 'tile')
Inputs may be any that keep to these rules, and one draw needn't show every extreme that they name: Every entry is 0 or 1; the middle entry pattern[j, b, 1] is 1; pattern[j, 0, 0] and pattern[j, 15, 2] are 0. `local_inv`: each matrix is symmetric. `seed_inv`: each matrix is symmetric.
All inputs are finite; a program needn't handle non-finite values.
Results may differ from a plain program's by a relative error of at most 0.0003.
Values sent between devices are 32-bit elements; how exact they have to be, the bound alone decides.
A program may use at most 128 MiB of HBM per device.

v0:
```python
import functools

import jax
import jax.numpy as jnp
from jax import lax
from jax.experimental import pallas as pl
from jax.experimental.pallas import tpu as pltpu
from jax.sharding import PartitionSpec as P

F32 = jnp.float32
BF16 = jnp.bfloat16
MESH = pl.DeviceIdType.MESH


def split(value):
    high = value.astype(BF16)
    return high, (value - high.astype(F32)).astype(BF16)


def dot(a, b):
    return lax.dot_general(a, b, (((1,), (0,)), ((), ())), preferred_element_type=F32)


def split_dot(a_high, a_low, b_high, b_low):
    return dot(a_high, b_high) + (dot(a_high, b_low) + dot(a_low, b_high))


def kernel(parts, ranks, local_ref, seed_ref, band_ref, pattern_ref, out_ref, var_ref,
           nxt, odd, wbuf, m_high, m_low, loc, wc_high, wc_low, wt_high, wt_low,
           wsend, wrecv, nsend, nrecv, hsend, hrecv, lsem):
    p, t = lax.axis_index("tm"), lax.axis_index("tile")
    rows, width = seed_ref.shape[1], seed_ref.shape[2]
    tiles, tr = wbuf.shape[1] // 3, wbuf.shape[3]
    lt = width // tr
    g = 2 if lt % 2 == 0 else 1
    span = (g + 2) * tr
    inner = pl.ds(tr, width)
    left_halo, right_halo = pl.ds(0, tr), pl.ds(tr + width, tr)
    has_right, has_left = t < ranks - 1, t > 0
    has_next = p < parts - 1

    barrier = pltpu.get_barrier_semaphore()
    around = [(a, b) for a in (-1, 0, 1) for b in (-1, 0, 1) if (a, b) != (0, 0)]

    def present(a, b):
        return (p + a >= 0) & (p + a < parts) & (t + b >= 0) & (t + b < ranks)

    for a, b in around:
        @pl.when(present(a, b))
        def _(a=a, b=b):
            pl.semaphore_signal(barrier, inc=1, device_id={"tm": p + a, "tile": t + b}, device_id_type=MESH)
    near_tm = 1 + jnp.where(p > 0, 1, 0) + jnp.where(p < parts - 1, 1, 0)
    near_tile = 1 + jnp.where(t > 0, 1, 0) + jnp.where(t < ranks - 1, 1, 0)
    pl.semaphore_wait(barrier, near_tm * near_tile - 1)

    def toward(d):
        return (1, has_right) if d == 0 else (-1, has_left)

    def with_w(j, d, k, incoming, action):
        step, _ = toward(d)
        owner = t - step * k
        at_end = owner == (0 if d == 0 else ranks - 1)
        for condition, skip in ((at_end, 1), (jnp.logical_not(at_end), 0)):
            @pl.when(condition)
            def _(skip=skip):
                part = wbuf.at[j, pl.ds(owner * lt * 3 + (skip if d == 0 else 0), lt * 3 - skip)]
                action(pltpu.make_async_remote_copy(
                    src_ref=part, dst_ref=part,
                    send_sem=wsend.at[j, d, k], recv_sem=wrecv.at[j, d, k if incoming else k + 1],
                    device_id={"tile": t - step if incoming else t + step}, device_id_type=MESH))

    def comes(d, k):
        return t - k >= 0 if d == 0 else t + k < ranks

    def start_own(j):
        for d in (1, 0):
            @pl.when(toward(d)[1])
            def _(d=d):
                with_w(j, d, 0, False, lambda copy: copy.start())

    def receive(j, k):
        for d in (1, 0):
            @pl.when(comes(d, k))
            def _(d=d):
                with_w(j, d, k, True, lambda copy: copy.wait_recv())

                @pl.when(toward(d)[1])
                def _():
                    with_w(j, d, k, False, lambda copy: copy.start())

    def block(u):
        return pl.ds(u * width, width)

    def seed_copy(index, u):
        if index == 0:
            src, dst, target = seed_ref.at[0], nxt.at[:, inner], t
        elif index == 1:
            src, dst, target = seed_ref.at[0, block(u), pl.ds(width - tr, tr)], nxt.at[block(u), left_halo], t + 1
        else:
            src, dst, target = seed_ref.at[0, block(u), pl.ds(0, tr)], nxt.at[block(u), right_halo], t - 1
        return pltpu.make_async_remote_copy(
            src_ref=src, dst_ref=dst, send_sem=nsend.at[index, u], recv_sem=nrecv.at[index, u],
            device_id={"tm": p - 1, "tile": target}, device_id_type=MESH)

    def halo_copy(d, u):
        if d == 0:
            src, dst, target = odd.at[block(u), pl.ds(width, tr)], odd.at[block(u), left_halo], t + 1
        else:
            src, dst, target = odd.at[block(u), pl.ds(tr, tr)], odd.at[block(u), right_halo], t - 1
        return pltpu.make_async_remote_copy(
            src_ref=src, dst_ref=dst, send_sem=hsend.at[d, u], recv_sem=hrecv.at[d, u],
            device_id={"tile": target}, device_id_type=MESH)

    def blocks_but(skipped, does, action):
        @pl.loop(0, ranks)
        def _(u):
            @pl.when(does & (u != skipped))
            def _():
                action(u)

    def mirror(field):
        for does, row, place in ((has_left, t * width - tr, left_halo), (has_right, (t + 1) * width, right_halo)):
            @pl.when(does)
            def _(row=row, place=place):
                for i in range(lt):
                    tile = field[pl.ds(pl.multiple_of(row, tr), tr), pl.ds(tr + i * tr, tr)]
                    field[pl.ds(pl.multiple_of(t * width + i * tr, tr), tr), place] = tile.T

    own_local = [pltpu.make_async_copy(band_ref.at[j], wbuf.at[j, pl.ds(t * lt * 3, lt * 3)], lsem.at[j]) for j in (0, 1)]
    locals_in = pltpu.make_async_copy(local_ref, loc, lsem.at[2])
    for copy in own_local[::-1]:
        copy.start()
    blocks_but(t + 1, (p > 0) & has_right, lambda u: seed_copy(1, u).start())
    blocks_but(t - 1, (p > 0) & has_left, lambda u: seed_copy(2, u).start())

    @pl.when(p > 0)
    def _():
        seed_copy(0, 0).start()

    locals_in.start()
    for j in (1, 0):
        own_local[j].wait()
        for b in range(lt):
            for k in range(3):
                at = (j, (t * lt + b) * 3 + k)
                wbuf[at] = wbuf[at] * pattern_ref[k, j, b].astype(F32)

    zero_halo = jnp.zeros((rows, tr), F32)
    for missing, place in ((t == 0, left_halo), (t == ranks - 1, right_halo)):
        @pl.when(missing)
        def _(place=place):
            odd[:, place] = zero_halo

            @pl.when(has_next)
            def _():
                nxt[:, place] = zero_halo

    @pl.when(p == parts - 1)
    def _():
        nxt[...] = jnp.zeros_like(nxt)

    for ref in (m_high, m_low):
        ref[pl.ds(0, tr), :] = jnp.zeros((tr, width), BF16)
        ref[pl.ds(tr + rows, tr), :] = jnp.zeros((tr, width), BF16)
    for j in (0, 1):
        @pl.when(has_left)
        def _(j=j):
            wbuf[j, 0] = jnp.zeros((tr, tr), F32)

        @pl.when(has_right)
        def _(j=j):
            wbuf[j, tiles * 3 - 1] = jnp.zeros((tr, tr), F32)

    for ref in (wc_high, wc_low, wt_high, wt_low):
        ref[...] = jnp.zeros_like(ref)
    start_own(1)
    start_own(0)

    chunk = 256

    def column_product(field, j):
        for i in range(lt // g):
            for c in range(g):
                for k in range(3):
                    high, low = split(wbuf[j, (t * lt + i * g + c) * 3 + k])
                    at = (i, pl.ds((c + k) * tr, tr), pl.ds(c * tr, tr))
                    wc_high[at] = high
                    wc_low[at] = low

        @pl.loop(0, rows // chunk)
        def _(r):
            start = pl.multiple_of(r * chunk, chunk)
            for i in range(lt // g):
                high, low = split(field[pl.ds(start, chunk), pl.ds(i * g * tr, span)])
                value = split_dot(high, low, wc_high[i], wc_low[i])
                at = (pl.ds(pl.multiple_of(start + tr, tr), chunk), pl.ds(i * g * tr, g * tr))
                high, low = split(value)
                m_high[at] = high
                m_low[at] = low

    def left_rows(j, owner, target, columns):
        @pl.loop(0, lt // g)
        def _(i):
            first = owner * lt + i * g
            for c in range(g):
                for k in range(3):
                    high, low = split(wbuf[j, (first + c) * 3 + k].T)
                    at = (pl.ds(c * tr, tr), pl.ds((c + k) * tr, tr))
                    wt_high[at] = high
                    wt_low[at] = low
            start = pl.multiple_of(first * tr, tr)
            source = pl.ds(start, span)
            value = split_dot(wt_high[...], wt_low[...], m_high[source, :], m_low[source, :])
            place = pl.ds(start, g * tr)
            target[place, columns] = loc[j, place, :].astype(F32) + value

    def left_round(j, k, target, columns):
        for d in (1, 0):
            @pl.when(comes(d, k))
            def _(d=d):
                left_rows(j, t - k if d == 0 else t + k, target, columns)

    def diagonal(index, field, offset):
        eye = lax.broadcasted_iota(jnp.int32, (tr, tr), 0) == lax.broadcasted_iota(jnp.int32, (tr, tr), 1)
        for c in range(lt):
            tile = field[pl.ds(pl.multiple_of(t * width + c * tr, tr), tr), pl.ds(offset + c * tr, tr)]
            var_ref[pl.ds(index, 1), pl.ds(c * tr, tr)] = jnp.sum(jnp.where(eye, tile, 0.0), axis=0, keepdims=True)

    receive(1, 1)
    receive(0, 1)

    @pl.when(has_next)
    def _():
        seed_copy(0, 0).wait_recv()

    blocks_but(t, has_next & has_left, lambda u: seed_copy(1, u).wait_recv())
    blocks_but(t, has_next & has_right, lambda u: seed_copy(2, u).wait_recv())
    mirror(nxt)
    column_product(nxt, 1)
    locals_in.wait()
    left_rows(1, t, odd, inner)
    left_round(1, 1, odd, inner)

    @pl.loop(2, ranks)
    def _(k):
        receive(1, k)
        left_round(1, k, odd, inner)

    diagonal(1, odd, tr)
    mirror(odd)
    blocks_but(t - 1, has_left, lambda u: halo_copy(1, u).start())
    blocks_but(t + 1, has_right, lambda u: halo_copy(0, u).start())

    @pl.loop(2, ranks - 1)
    def _(k):
        receive(0, k)

    blocks_but(t, has_left, lambda u: halo_copy(0, u).wait_recv())
    blocks_but(t, has_right, lambda u: halo_copy(1, u).wait_recv())
    column_product(odd, 0)
    everything = pl.ds(0, width)
    left_rows(0, t, out_ref, everything)

    @pl.loop(1, ranks - 1)
    def _(k):
        left_round(0, k, out_ref, everything)

    if ranks > 2:
        receive(0, ranks - 1)
    left_round(0, ranks - 1, out_ref, everything)
    diagonal(0, out_ref, 0)

    for j in (1, 0):
        for d in (1, 0):
            @pl.when(toward(d)[1])
            def _(j=j, d=d):
                with_w(j, d, 0, False, lambda copy: copy.wait_send())

                @pl.loop(1, ranks - 1)
                def _(k):
                    @pl.when(comes(d, k))
                    def _():
                        with_w(j, d, k, False, lambda copy: copy.wait_send())
    @pl.when(p > 0)
    def _():
        seed_copy(0, 0).wait_send()

    blocks_but(t + 1, (p > 0) & has_right, lambda u: seed_copy(1, u).wait_send())
    blocks_but(t - 1, (p > 0) & has_left, lambda u: seed_copy(2, u).wait_send())
    blocks_but(t + 1, has_right, lambda u: halo_copy(0, u).wait_send())
    blocks_but(t - 1, has_left, lambda u: halo_copy(1, u).wait_send())


def per_device(parts, ranks, local_inv, seed_inv, band, pattern):
    rows, width = seed_inv.shape[1:]
    lt, tr = band.shape[1], band.shape[3]
    tiles = rows // tr
    g = 2 if lt % 2 == 0 else 1
    span = (g + 2) * tr
    dma = pltpu.SemaphoreType.DMA
    out, var = pl.pallas_call(
        functools.partial(kernel, parts, ranks),
        out_shape=(pltpu.VMEM((rows, width), F32), pltpu.VMEM((2, width), F32)),
        in_specs=[pl.BlockSpec(memory_space=pltpu.HBM)] * 3 + [pl.BlockSpec(memory_space=pltpu.SMEM)],
        out_specs=(pl.BlockSpec(memory_space=pltpu.VMEM), pl.BlockSpec(memory_space=pltpu.VMEM)),
        scratch_shapes=[
            pltpu.VMEM((rows, width + 2 * tr), F32),
            pltpu.VMEM((rows, width + 2 * tr), F32),
            pltpu.VMEM((2, tiles * 3, tr, tr), F32),
            pltpu.VMEM((rows + 2 * tr, width), BF16),
            pltpu.VMEM((rows + 2 * tr, width), BF16),
            pltpu.VMEM((2, rows, width), BF16),
            pltpu.VMEM((lt // g, span, g * tr), BF16),
            pltpu.VMEM((lt // g, span, g * tr), BF16),
            pltpu.VMEM((g * tr, span), BF16),
            pltpu.VMEM((g * tr, span), BF16),
            dma((2, 2, ranks + 1)),
            dma((2, 2, ranks + 1)),
            dma((3, ranks)),
            dma((3, ranks)),
            dma((2, ranks)),
            dma((2, ranks)),
            dma((3,)),
        ],
        compiler_params=pltpu.CompilerParams(
            collective_id=0, has_side_effects=True, vmem_limit_bytes=58 * 1024 * 1024
        ),
    )(local_inv, seed_inv, band.reshape(2, lt * 3, tr, tr), pattern.transpose(2, 0, 1))
    return out[None], var


def solution(mesh):
    placed = (
        P("tm", None, "tile"),
        P("tm", None, "tile"),
        P("tm", "tile", None, None, None),
        P("tm", "tile", None),
    )
    return jax.shard_map(
        functools.partial(per_device, mesh.shape["tm"], mesh.shape["tile"]),
        mesh=mesh,
        in_specs=placed,
        out_specs=(P("tm", None, "tile"), P("tm", "tile")),
        check_vma=False,
    )
```

profile of v0, /device:TPU:5, one launch (start us, length us, event | category | flops | bytes accessed | tf_op | source)
XLA Modules:
  0.0 143.8 jit_solution(5923009117954652406)
XLA Ops:
  0.6 140.5 %shard_map.59 = (f32[2048,512]{1,0:T(8,128)S(1)}, f32[2,512]{1,0:T(2,128)S(1)}) custom-call(bf16[2,2048,512]{2,1,0:T(8,128)(2,1)} %local_ref.1, f32[1,2048,512]{2,1,0:T(8,128)} %seed_ref.1, f32[2,12,128,128]{3,2,1,0:T(8,128)} %bitcast.4, s32[3,2,4]{2,1,0:T(2,128)} %bitcast.5), custom_call_target="tpu_custom_call" | custom-call | tf_op jit(solution)/shard_map/pallas_call | solution.py:301
  141.2 2.0 %copy.8 = f32[1,2048,512]{2,1,0:T(8,128)} copy(f32[1,2048,512]{2,1,0:T(8,128)S(1)} %bitcast.3) | data formatting | bytes 8388608
  143.2 0.6 copy.9
where the time goes:
time: 144 us
  Pallas kernels  141 us (98%)
  local copies, waits for them, and re-layouts  2.61 us (2%)
    pallas_call x1, Pallas kernels, per_device(): pl.pallas_call(functools.partial(kernel, parts, ranks), out_shape=(pltpu....  141 us

commit v1 on v0

v1 whole, which is shorter than its diff:
```python
import functools

import jax
import jax.numpy as jnp
from jax import lax
from jax.experimental import pallas as pl
from jax.experimental.pallas import tpu as pltpu
from jax.sharding import PartitionSpec as P

F32 = jnp.float32
BF16 = jnp.bfloat16
MESH = pl.DeviceIdType.MESH


def split(value):
    high = value.astype(BF16)
    return high, (value - high.astype(F32)).astype(BF16)


def dot(a, b):
    return lax.dot_general(a, b, (((1,), (0,)), ((), ())), preferred_element_type=F32)


def split_dot(a_high, a_low, b_high, b_low):
    return dot(a_high, b_high) + (dot(a_high, b_low) + dot(a_low, b_high))


def kernel(parts, ranks, local_ref, seed_ref, band_ref, pattern_ref, out_ref, var_ref,
           nxt, odd, wbuf, m_high, m_low, loc, wc_high, wc_low, wt_high, wt_low,
           wsend, wrecv, nsend, nrecv, hsend, hrecv, rsend, rrecv, lsem):
    p, t = lax.axis_index("tm"), lax.axis_index("tile")
    rows, width = seed_ref.shape[1], seed_ref.shape[2]
    tr = wbuf.shape[3]
    lt = width // tr
    g = 2 if lt % 2 == 0 else 1
    span = (g + 2) * tr
    chunk = 256 if width % 256 == 0 else tr
    inner = pl.ds(tr, width)
    everything = pl.ds(0, width)
    has_next = p < parts - 1

    barrier = pltpu.get_barrier_semaphore()

    @pl.loop(0, ranks)
    def _(u):
        @pl.when(u != t)
        def _():
            pl.semaphore_signal(barrier, inc=1, device_id={"tile": u}, device_id_type=MESH)

    for a in (-1, 1):
        for b in (-1, 0, 1):
            @pl.when((p + a >= 0) & (p + a < parts) & (t + b >= 0) & (t + b < ranks))
            def _(a=a, b=b):
                pl.semaphore_signal(barrier, inc=1, device_id={"tm": p + a, "tile": t + b}, device_id_type=MESH)
    near_tm = jnp.where(p > 0, 1, 0) + jnp.where(p < parts - 1, 1, 0)
    near_tile = 1 + jnp.where(t > 0, 1, 0) + jnp.where(t < ranks - 1, 1, 0)
    pl.semaphore_wait(barrier, ranks - 1 + near_tm * near_tile)

    def block(u):
        return pl.ds(pl.multiple_of(u * width, width), width)

    def tile(b):
        return pl.ds(pl.multiple_of(b * tr, tr), tr)

    def triangle(s):
        behind, ahead = t - s, t + s
        count = ranks - 1 - t if s > 0 else t
        has_behind, has_ahead = (t > 0, t < ranks - 1) if s > 0 else (t < ranks - 1, t > 0)
        first, last = pl.ds(tr, tr), pl.ds(width, tr)
        left, right = pl.ds(0, tr), pl.ds(tr + width, tr)
        edge_behind, edge_ahead = (first, last) if s > 0 else (last, first)
        halo_behind, halo_ahead = (left, right) if s > 0 else (right, left)
        tile_behind, tile_ahead = (t * lt - 1, (t + 1) * lt) if s > 0 else ((t + 1) * lt, t * lt - 1)
        tile_corner = (t + 1) * lt - 1 if s > 0 else t * lt

        def groups(base, start, does, action):
            number = ranks - 1 - base if s > 0 else base

            @pl.when(does)
            def _():
                @pl.loop(start, number + 1)
                def _(k):
                    action(base + s * k)


        def w_copy(j, u):
            part = wbuf.at[j, pl.ds(u * lt * 3, lt * 3)]
            return pltpu.make_async_remote_copy(
                src_ref=part, dst_ref=part, send_sem=wsend.at[j, u], recv_sem=wrecv.at[j, u],
                device_id={"tile": behind}, device_id_type=MESH)

        def pass_on(j):
            def one(u):
                w_copy(j, u).wait_recv()
                w_copy(j, u).start()
            groups(t, 1, has_behind, one)

        def arrive(j, u):
            @pl.when(jnp.logical_not(has_behind))
            def _():
                w_copy(j, u).wait_recv()


        def seed_copy(src, dst, kind, u, target):
            return pltpu.make_async_remote_copy(
                src_ref=seed_ref.at[(0,) + src], dst_ref=nxt.at[dst],
                send_sem=nsend.at[kind, u], recv_sem=nrecv.at[kind, u],
                device_id={"tm": p - 1, "tile": target}, device_id_type=MESH)

        def seeds(action):
            low, high = pl.ds(0, tr), pl.ds(width - tr, tr)
            toward, back = (low, high) if s > 0 else (high, low)
            sends = p > 0
            number = t if s > 0 else ranks - 1 - t

            def walk(start, does, one):
                @pl.when(does)
                def _():
                    @pl.loop(start, number + 1)
                    def _(k):
                        one(t - s * k)

            walk(0, sends & has_ahead, lambda u: action(
                seed_copy((block(u), back), (block(u), halo_behind), 2, u, ahead)))
            walk(2, sends & has_behind, lambda u: action(
                seed_copy((block(u), toward), (block(u), halo_ahead), 1, u, behind)))

            @pl.when(sends & has_behind)
            def _():
                corner = tile(t * lt if s > 0 else (t + 1) * lt - 1)
                action(seed_copy((corner, toward), (corner, halo_ahead), 4, 0, behind))

            @pl.when(sends & has_ahead)
            def _():
                row = tile(tile_ahead)
                action(seed_copy((row, everything), (row, inner), 3, 0, t))
            walk(0, sends, lambda u: action(seed_copy((block(u), everything), (block(u), inner), 0, u, t)))

        def seed_arrived(dst, kind, u):
            pltpu.make_async_remote_copy(
                src_ref=nxt.at[dst], dst_ref=nxt.at[dst], send_sem=nsend.at[kind, u], recv_sem=nrecv.at[kind, u],
                device_id={"tile": behind}, device_id_type=MESH).wait_recv()

        def halo_copy(place, source, target_place, kind, u, target):
            return pltpu.make_async_remote_copy(
                src_ref=odd.at[place, source], dst_ref=odd.at[place, target_place],
                send_sem=hsend.at[kind, u], recv_sem=hrecv.at[kind, u],
                device_id={"tile": target}, device_id_type=MESH)

        def halo_ahead_copy(u):
            return halo_copy(block(u), edge_ahead, halo_behind, 0, u, ahead)

        def halo_corner_copy(b):
            return halo_copy(tile(b), edge_ahead, halo_behind, 2, 0, ahead)

        def halo_behind_copy(u):
            return halo_copy(block(u), edge_behind, halo_ahead, 1, u, behind)

        def result_copy(u):
            return pltpu.make_async_remote_copy(
                src_ref=nxt.at[block(u), inner], dst_ref=out_ref.at[block(t), everything],
                send_sem=rsend.at[u], recv_sem=rrecv.at[t],
                device_id={"tile": u}, device_id_type=MESH)

        def result_arrived(u):
            pltpu.make_async_remote_copy(
                src_ref=nxt.at[block(u), inner], dst_ref=out_ref.at[block(u), everything],
                send_sem=rsend.at[u], recv_sem=rrecv.at[u],
                device_id={"tile": behind}, device_id_type=MESH).wait_recv()

        def clear_halo(field, does):
            for missing, place in ((has_behind, halo_behind), (has_ahead, halo_ahead)):
                @pl.when(jnp.logical_not(missing) & does)
                def _(place=place):
                    field[:, place] = jnp.zeros((rows, tr), F32)

        def own_tile(i):
            return tile(t * lt + i)

        def mirror_ahead(field):
            @pl.when(has_ahead)
            def _():
                for i in range(lt):
                    field[own_tile(i), halo_ahead] = field[tile(tile_ahead), pl.ds(tr + i * tr, tr)].T

            @pl.when(has_ahead & has_behind)
            def _():
                field[tile(tile_behind), halo_ahead] = field[tile(tile_ahead), halo_behind].T

        def column_product(field, j):
            for i in range(lt // g):
                for c in range(g):
                    for k in range(3):
                        high, low = split(wbuf[j, (t * lt + i * g + c) * 3 + k])
                        at = (i, pl.ds((c + k) * tr, tr), pl.ds(c * tr, tr))
                        wc_high[at] = high
                        wc_low[at] = low

            def some_rows(start, size):
                for i in range(lt // g):
                    high, low = split(field[pl.ds(start, size), pl.ds(i * g * tr, span)])
                    value = split_dot(high, low, wc_high[i], wc_low[i])
                    at = (pl.ds(pl.multiple_of(start + tr, tr), size), pl.ds(i * g * tr, g * tr))
                    high, low = split(value)
                    m_high[at] = high
                    m_low[at] = low

            @pl.when(has_behind)
            def _():
                some_rows(pl.multiple_of(tile_behind * tr, tr), tr)

            base = t * width if s > 0 else 0

            @pl.loop(0, (count + 1) * (width // chunk))
            def _(r):
                some_rows(pl.multiple_of(base + r * chunk, chunk), chunk)

        def left_rows(j, owner, target, columns, turned):
            @pl.loop(0, lt // g)
            def _(i):
                begin = owner * lt + i * g
                for c in range(g):
                    for k in range(3):
                        high, low = split(wbuf[j, (begin + c) * 3 + k].T)
                        at = (pl.ds(c * tr, tr), pl.ds((c + k) * tr, tr))
                        wt_high[at] = high
                        wt_low[at] = low
                start = pl.multiple_of(begin * tr, tr)
                source = pl.ds(start, span)
                value = split_dot(wt_high[...], wt_low[...], m_high[source, :], m_low[source, :])
                place = pl.ds(start, g * tr)
                value = loc[j, place, :].astype(F32) + value
                target[place, columns] = value
                if turned:
                    for c in range(g):
                        lanes = pl.ds(pl.multiple_of(tr + (i * g + c) * tr, tr), tr)
                        for q in range(lt):
                            nxt[tile(owner * lt + q), lanes] = value[c * tr:(c + 1) * tr, q * tr:(q + 1) * tr].T

        def diagonal(index, field, offset):
            eye = lax.broadcasted_iota(jnp.int32, (tr, tr), 0) == lax.broadcasted_iota(jnp.int32, (tr, tr), 1)
            for c in range(lt):
                part = field[own_tile(c), pl.ds(offset + c * tr, tr)]
                var_ref[pl.ds(index, 1), pl.ds(c * tr, tr)] = jnp.sum(jnp.where(eye, part, 0.0), axis=0, keepdims=True)

        own_local = [pltpu.make_async_copy(band_ref.at[j], wbuf.at[j, pl.ds(t * lt * 3, lt * 3)], lsem.at[j]) for j in (0, 1)]
        locals_in = pltpu.make_async_copy(local_ref, loc, lsem.at[2])
        for copy in own_local[::-1]:
            copy.start()
        seeds(lambda copy: copy.start())
        locals_in.start()

        def own_factor(j):
            own_local[j].wait()
            for b in range(lt):
                for k in range(3):
                    at = (j, (t * lt + b) * 3 + k)
                    wbuf[at] = wbuf[at] * pattern_ref[k, j, b].astype(F32)

        own_factor(1)

        @pl.when(has_behind)
        def _():
            w_copy(1, t).start()

        own_factor(0)
        clear_halo(odd, True)
        clear_halo(nxt, has_next)

        @pl.when(p == parts - 1)
        def _():
            nxt[...] = jnp.zeros_like(nxt)

        for ref in (m_high, m_low):
            ref[pl.ds(0, tr), :] = jnp.zeros((tr, width), BF16)
            ref[pl.ds(tr + rows, tr), :] = jnp.zeros((tr, width), BF16)
        for ref in (wc_high, wc_low, wt_high, wt_low):
            ref[...] = jnp.zeros_like(ref)

        pass_on(1)

        @pl.when(has_behind)
        def _():
            w_copy(0, t).start()

        if s < 0:
            pass_on(0)

        groups(t, 1, has_next & has_behind, lambda u: seed_arrived((block(u), halo_behind), 1, u))
        groups(t, 1, has_next & has_ahead, lambda u: seed_arrived((block(u), halo_ahead), 2, u))

        @pl.when(has_next & has_behind)
        def _():
            seed_arrived((tile(tile_behind), halo_behind), 4, 0)
            seed_arrived((tile(tile_behind), inner), 3, 0)
        groups(t, 0, has_next, lambda u: seed_arrived((block(u), inner), 0, u))

        @pl.when(has_behind)
        def _():
            for i in range(lt):
                nxt[own_tile(i), halo_behind] = nxt[tile(tile_behind), pl.ds(tr + i * tr, tr)].T
        mirror_ahead(nxt)
        column_product(nxt, 1)
        locals_in.wait()
        left_rows(1, t, odd, inner, False)

        def odd_rows(u):
            arrive(1, u)
            left_rows(1, u, odd, inner, False)
        groups(t, 1, True, odd_rows)

        groups(t, 0, has_behind, lambda u: halo_behind_copy(u).start())

        @pl.when(has_ahead)
        def _():
            halo_corner_copy(tile_corner).start()
        groups(t, 1, has_ahead, lambda u: halo_ahead_copy(u).start())
        if s > 0:
            pass_on(0)
        diagonal(1, odd, tr)
        mirror_ahead_own = has_ahead

        @pl.when(has_behind)
        def _():
            halo_corner_copy(tile_behind).wait_recv()
        groups(t, 0, has_behind, lambda u: halo_ahead_copy(u).wait_recv())
        groups(t, 1, has_ahead, lambda u: halo_behind_copy(u).wait_recv())

        @pl.when(has_behind)
        def _():
            for i in range(lt):
                odd[tile(tile_behind), pl.ds(tr + i * tr, tr)] = odd[own_tile(i), halo_behind].T
        mirror_ahead(odd)
        column_product(odd, 0)
        left_rows(0, t, out_ref, everything, False)
        diagonal(0, out_ref, 0)

        def first_rows(u):
            arrive(0, u)
            left_rows(0, u, out_ref, everything, True)
            result_copy(u).start()
        groups(t, 1, True, first_rows)

        @pl.when(has_behind)
        def _():
            @pl.loop(1, ranks - count)
            def _(k):
                result_arrived(t - s * k)

        for j in (1, 0):
            groups(t, 0, has_behind, lambda u, j=j: w_copy(j, u).wait_send())
        seeds(lambda copy: copy.wait_send())
        groups(t, 0, has_behind, lambda u: halo_behind_copy(u).wait_send())

        @pl.when(has_ahead)
        def _():
            halo_corner_copy(tile_corner).wait_send()
        groups(t, 1, has_ahead, lambda u: halo_ahead_copy(u).wait_send())
        groups(t, 1, True, lambda u: result_copy(u).wait_send())

    for remainder, s in ((0, 1), (1, -1)):
        @pl.when(lax.rem(p, 2) == remainder)
        def _(s=s):
            triangle(s)


def per_device(parts, ranks, local_inv, seed_inv, band, pattern):
    rows, width = seed_inv.shape[1:]
    lt, tr = band.shape[1], band.shape[3]
    tiles = rows // tr
    g = 2 if lt % 2 == 0 else 1
    span = (g + 2) * tr
    dma = pltpu.SemaphoreType.DMA
    out, var = pl.pallas_call(
        functools.partial(kernel, parts, ranks),
        out_shape=(pltpu.VMEM((rows, width), F32), pltpu.VMEM((2, width), F32)),
        in_specs=[pl.BlockSpec(memory_space=pltpu.HBM)] * 3 + [pl.BlockSpec(memory_space=pltpu.SMEM)],
        out_specs=(pl.BlockSpec(memory_space=pltpu.VMEM), pl.BlockSpec(memory_space=pltpu.VMEM)),
        scratch_shapes=[
            pltpu.VMEM((rows, width + 2 * tr), F32),
            pltpu.VMEM((rows, width + 2 * tr), F32),
            pltpu.VMEM((2, tiles * 3, tr, tr), F32),
            pltpu.VMEM((rows + 2 * tr, width), BF16),
            pltpu.VMEM((rows + 2 * tr, width), BF16),
            pltpu.VMEM((2, rows, width), BF16),
            pltpu.VMEM((lt // g, span, g * tr), BF16),
            pltpu.VMEM((lt // g, span, g * tr), BF16),
            pltpu.VMEM((g * tr, span), BF16),
            pltpu.VMEM((g * tr, span), BF16),
            dma((2, ranks)),
            dma((2, ranks)),
            dma((5, ranks)),
            dma((5, ranks)),
            dma((3, ranks)),
            dma((3, ranks)),
            dma((ranks,)),
            dma((ranks,)),
            dma((3,)),
        ],
        compiler_params=pltpu.CompilerParams(
            collective_id=0, has_side_effects=True, vmem_limit_bytes=58 * 1024 * 1024
        ),
    )(local_inv, seed_inv, band.reshape(2, lt * 3, tr, tr), pattern.transpose(2, 0, 1))
    return out[None], var


def solution(mesh):
    placed = (
        P("tm", None, "tile"),
        P("tm", None, "tile"),
        P("tm", "tile", None, None, None),
        P("tm", "tile", None),
    )
    return jax.shard_map(
        functools.partial(per_device, mesh.shape["tm"], mesh.shape["tile"]),
        mesh=mesh,
        in_specs=placed,
        out_specs=(P("tm", None, "tile"), P("tm", "tile")),
        check_vma=False,
    )
```

time: 144 us -> 158 us (1.097)
  the two profiles are of different devices: /device:TPU:5 before, /device:TPU:1 now
where the time goes in v1:
time: 158 us
  Pallas kernels  154 us (97%)
  local copies, waits for them, and re-layouts  2.61 us (2%)
    pallas_call x1, Pallas kernels, per_device(): pl.pallas_call(functools.partial(kernel, parts, ranks), out_shape=(pltpu....  154 us

profile of v1, /device:TPU:1, one launch (start us, length us, event | category | flops | bytes accessed | tf_op | source)
XLA Modules:
  0.0 157.6 jit_solution(5101503673489606745)
XLA Ops:
  0.6 154.4 %shard_map.59 = (f32[2048,512]{1,0:T(8,128)S(1)}, f32[2,512]{1,0:T(2,128)S(1)}) custom-call(bf16[2,2048,512]{2,1,0:T(8,128)(2,1)} %local_ref.1, f32[1,2048,512]{2,1,0:T(8,128)} %seed_ref.1, f32[2,12,128,128]{3,2,1,0:T(8,128)} %bitcast.4, s32[3,2,4]{2,1,0:T(2,128)} %bitcast.5), custom_call_target="tpu_custom_call" | custom-call | tf_op jit(solution)/shard_map/pallas_call | solution.py:374
  155.0 2.0 %copy.8 = f32[1,2048,512]{2,1,0:T(8,128)} copy(f32[1,2048,512]{2,1,0:T(8,128)S(1)} %bitcast.3) | data formatting | bytes 8388608
  157.0 0.6 copy.9

commit v2 on v1

--- a/solution.py
+++ b/solution.py
@@ -27,7 +27,7 @@
 
 def kernel(parts, ranks, local_ref, seed_ref, band_ref, pattern_ref, out_ref, var_ref,
            nxt, odd, wbuf, m_high, m_low, loc, wc_high, wc_low, wt_high, wt_low,
-           wsend, wrecv, nsend, nrecv, hsend, hrecv, rsend, rrecv, lsem):
+           wsend, wrecv, nsend, nrecv, hsend, hrecv, rsend, rrecv, lsem, go):
     p, t = lax.axis_index("tm"), lax.axis_index("tile")
     rows, width = seed_ref.shape[1], seed_ref.shape[2]
     tr = wbuf.shape[3]
@@ -41,20 +41,52 @@
 
     barrier = pltpu.get_barrier_semaphore()
 
+    paired = parts % 2 == 0
+    partner = p + 1 - 2 * lax.rem(p, 2)
+
+    def greet(q, u):
+        pl.semaphore_signal(barrier, inc=1, device_id={"tm": q, "tile": u}, device_id_type=MESH)
+
     @pl.loop(0, ranks)
     def _(u):
         @pl.when(u != t)
         def _():
-            pl.semaphore_signal(barrier, inc=1, device_id={"tile": u}, device_id_type=MESH)
+            greet(p, u)
+        if paired:
+            greet(partner, u)
 
     for a in (-1, 1):
         for b in (-1, 0, 1):
-            @pl.when((p + a >= 0) & (p + a < parts) & (t + b >= 0) & (t + b < ranks))
+            meet = (p + a >= 0) & (p + a < parts) & (t + b >= 0) & (t + b < ranks)
+
+            @pl.when(meet & (p + a != partner) if paired else meet)
             def _(a=a, b=b):
-                pl.semaphore_signal(barrier, inc=1, device_id={"tm": p + a, "tile": t + b}, device_id_type=MESH)
-    near_tm = jnp.where(p > 0, 1, 0) + jnp.where(p < parts - 1, 1, 0)
+                greet(p + a, t + b)
+    near_tm = jnp.where(p > 0, 1, 0) + jnp.where(p < parts - 1, 1, 0) - (1 if paired else 0)
     near_tile = 1 + jnp.where(t > 0, 1, 0) + jnp.where(t < ranks - 1, 1, 0)
-    pl.semaphore_wait(barrier, ranks - 1 + near_tm * near_tile)
+    meets = ranks - 1 + (ranks if paired else 0) + near_tm * near_tile
+    own_local = [pltpu.make_async_copy(band_ref.at[j], wbuf.at[j, pl.ds(t * lt * 3, lt * 3)], lsem.at[j]) for j in (0, 1)]
+    locals_in = pltpu.make_async_copy(local_ref, loc, lsem.at[2])
+    for copy in own_local[::-1]:
+        copy.start()
+    locals_in.start()
+
+    @pl.when(p == parts - 1)
+    def _():
+        nxt[...] = jnp.zeros_like(nxt)
+
+    for ref in (m_high, m_low):
+        ref[pl.ds(0, tr), :] = jnp.zeros((tr, width), BF16)
+        ref[pl.ds(tr + rows, tr), :] = jnp.zeros((tr, width), BF16)
+    for ref in (wc_high, wc_low, wt_high, wt_low):
+        ref[...] = jnp.zeros_like(ref)
+    for j in (1, 0):
+        own_local[j].wait()
+        for b in range(lt):
+            for k in range(3):
+                at = (j, (t * lt + b) * 3 + k)
+                wbuf[at] = wbuf[at] * pattern_ref[k, j, b].astype(F32)
+    pl.semaphore_wait(barrier, meets)
 
     def block(u):
         return pl.ds(pl.multiple_of(u * width, width), width)
@@ -89,11 +121,12 @@
                 src_ref=part, dst_ref=part, send_sem=wsend.at[j, u], recv_sem=wrecv.at[j, u],
                 device_id={"tile": behind}, device_id_type=MESH)
 
+        def pass_one(j, u):
+            w_copy(j, u).wait_recv()
+            w_copy(j, u).start()
+
         def pass_on(j):
-            def one(u):
-                w_copy(j, u).wait_recv()
-                w_copy(j, u).start()
-            groups(t, 1, has_behind, one)
+            groups(t, 1, has_behind, lambda u: pass_one(j, u))
 
         def arrive(j, u):
             @pl.when(jnp.logical_not(has_behind))
@@ -168,6 +201,18 @@
                 send_sem=rsend.at[u], recv_sem=rrecv.at[u],
                 device_id={"tile": behind}, device_id_type=MESH).wait_recv()
 
+        def signal_partner():
+            if paired:
+                @pl.loop(0, ranks)
+                def _(u):
+                    @pl.when(u != t)
+                    def _():
+                        pl.semaphore_signal(go, inc=1, device_id={"tm": partner, "tile": u}, device_id_type=MESH)
+
+        def wait_partner():
+            if paired:
+                pl.semaphore_wait(go, 1)
+
         def clear_halo(field, does):
             for missing, place in ((has_behind, halo_behind), (has_ahead, halo_ahead)):
                 @pl.when(jnp.logical_not(missing) & does)
@@ -187,7 +232,7 @@
             def _():
                 field[tile(tile_behind), halo_ahead] = field[tile(tile_ahead), halo_behind].T
 
-        def column_product(field, j):
+        def own_columns(j):
             for i in range(lt // g):
                 for c in range(g):
                     for k in range(3):
@@ -196,24 +241,25 @@
                         wc_high[at] = high
                         wc_low[at] = low
 
-            def some_rows(start, size):
-                for i in range(lt // g):
-                    high, low = split(field[pl.ds(start, size), pl.ds(i * g * tr, span)])
-                    value = split_dot(high, low, wc_high[i], wc_low[i])
-                    at = (pl.ds(pl.multiple_of(start + tr, tr), size), pl.ds(i * g * tr, g * tr))
-                    high, low = split(value)
-                    m_high[at] = high
-                    m_low[at] = low
-
+        def some_rows(field, start, size):
+            for i in range(lt // g):
+                high, low = split(field[pl.ds(start, size), pl.ds(i * g * tr, span)])
+                value = split_dot(high, low, wc_high[i], wc_low[i])
+                at = (pl.ds(pl.multiple_of(start + tr, tr), size), pl.ds(i * g * tr, g * tr))
+                high, low = split(value)
+                m_high[at] = high
+                m_low[at] = low
+
+        def group_rows(field, u):
+            @pl.loop(0, width // chunk)
+            def _(r):
+                some_rows(field, pl.multiple_of(u * width + r * chunk, chunk), chunk)
+
+        def near_rows(field):
             @pl.when(has_behind)
             def _():
-                some_rows(pl.multiple_of(tile_behind * tr, tr), tr)
-
-            base = t * width if s > 0 else 0
-
-            @pl.loop(0, (count + 1) * (width // chunk))
-            def _(r):
-                some_rows(pl.multiple_of(base + r * chunk, chunk), chunk)
+                some_rows(field, pl.multiple_of(tile_behind * tr, tr), tr)
+            group_rows(field, t)
 
         def left_rows(j, owner, target, columns, turned):
             @pl.loop(0, lt // g)
@@ -243,103 +289,146 @@
                 part = field[own_tile(c), pl.ds(offset + c * tr, tr)]
                 var_ref[pl.ds(index, 1), pl.ds(c * tr, tr)] = jnp.sum(jnp.where(eye, part, 0.0), axis=0, keepdims=True)
 
-        own_local = [pltpu.make_async_copy(band_ref.at[j], wbuf.at[j, pl.ds(t * lt * 3, lt * 3)], lsem.at[j]) for j in (0, 1)]
-        locals_in = pltpu.make_async_copy(local_ref, loc, lsem.at[2])
-        for copy in own_local[::-1]:
-            copy.start()
+        far_end = t + s * count
+
+        @pl.when(has_behind)
+        def _():
+            w_copy(1, t).start()
         seeds(lambda copy: copy.start())
-        locals_in.start()
-
-        def own_factor(j):
-            own_local[j].wait()
-            for b in range(lt):
-                for k in range(3):
-                    at = (j, (t * lt + b) * 3 + k)
-                    wbuf[at] = wbuf[at] * pattern_ref[k, j, b].astype(F32)
-
-        own_factor(1)
-
-        @pl.when(has_behind)
-        def _():
-            w_copy(1, t).start()
-
-        own_factor(0)
         clear_halo(odd, True)
         clear_halo(nxt, has_next)
-
-        @pl.when(p == parts - 1)
-        def _():
-            nxt[...] = jnp.zeros_like(nxt)
-
-        for ref in (m_high, m_low):
-            ref[pl.ds(0, tr), :] = jnp.zeros((tr, width), BF16)
-            ref[pl.ds(tr + rows, tr), :] = jnp.zeros((tr, width), BF16)
-        for ref in (wc_high, wc_low, wt_high, wt_low):
-            ref[...] = jnp.zeros_like(ref)
-
         pass_on(1)
 
         @pl.when(has_behind)
         def _():
             w_copy(0, t).start()
 
-        if s < 0:
-            pass_on(0)
-
-        groups(t, 1, has_next & has_behind, lambda u: seed_arrived((block(u), halo_behind), 1, u))
-        groups(t, 1, has_next & has_ahead, lambda u: seed_arrived((block(u), halo_ahead), 2, u))
+        def seeds_here(u):
+            @pl.when(has_next)
+            def _():
+                seed_arrived((block(u), inner), 0, u)
+                seed_arrived((block(u), halo_ahead), 2, u)
+
+            @pl.when(has_next & has_behind)
+            def _():
+                seed_arrived((block(u), halo_behind), 1, u)
+
+        @pl.when(has_next)
+        def _():
+            seed_arrived((block(t), inner), 0, t)
 
         @pl.when(has_next & has_behind)
         def _():
+            seed_arrived((tile(tile_behind), inner), 3, 0)
             seed_arrived((tile(tile_behind), halo_behind), 4, 0)
-            seed_arrived((tile(tile_behind), inner), 3, 0)
-        groups(t, 0, has_next, lambda u: seed_arrived((block(u), inner), 0, u))
+
+        @pl.when(has_ahead)
+        def _():
+            seeds_here(ahead)
 
         @pl.when(has_behind)
         def _():
             for i in range(lt):
                 nxt[own_tile(i), halo_behind] = nxt[tile(tile_behind), pl.ds(tr + i * tr, tr)].T
         mirror_ahead(nxt)
-        column_product(nxt, 1)
+        own_columns(1)
+        near_rows(nxt)
         locals_in.wait()
-        left_rows(1, t, odd, inner, False)
 
         def odd_rows(u):
-            arrive(1, u)
+            @pl.when(u != t)
+            def _():
+                arrive(1, u)
             left_rows(1, u, odd, inner, False)
-        groups(t, 1, True, odd_rows)
-
-        groups(t, 0, has_behind, lambda u: halo_behind_copy(u).start())
-
-        @pl.when(has_ahead)
-        def _():
-            halo_corner_copy(tile_corner).start()
-        groups(t, 1, has_ahead, lambda u: halo_ahead_copy(u).start())
+
+            @pl.when(has_behind)
+            def _():
+                halo_behind_copy(u).start()
+
+            @pl.when(has_ahead & (u == t))
+            def _():
+                halo_corner_copy(tile_corner).start()
+
+            @pl.when(u != t)
+            def _():
+                halo_ahead_copy(u).start()
+
+        def odd_step(u):
+            if s < 0:
+                @pl.when(has_behind)
+                def _():
+                    pass_one(0, u)
+
+            @pl.when(u != ahead)
+            def _():
+                seeds_here(u)
+            group_rows(nxt, u)
+            odd_rows(u - s)
+        groups(t, 1, has_ahead, odd_step)
+        odd_rows(far_end)
         if s > 0:
             pass_on(0)
         diagonal(1, odd, tr)
-        mirror_ahead_own = has_ahead
+
+        def halos_here(u):
+            halo_behind_copy(u).wait_recv()
+
+            @pl.when(has_behind)
+            def _():
+                halo_ahead_copy(u).wait_recv()
 
         @pl.when(has_behind)
         def _():
             halo_corner_copy(tile_behind).wait_recv()
-        groups(t, 0, has_behind, lambda u: halo_ahead_copy(u).wait_recv())
-        groups(t, 1, has_ahead, lambda u: halo_behind_copy(u).wait_recv())
+            halo_ahead_copy(t).wait_recv()
+
+        @pl.when(has_ahead)
+        def _():
+            halos_here(ahead)
 
         @pl.when(has_behind)
         def _():
             for i in range(lt):
                 odd[tile(tile_behind), pl.ds(tr + i * tr, tr)] = odd[own_tile(i), halo_behind].T
         mirror_ahead(odd)
-        column_product(odd, 0)
-        left_rows(0, t, out_ref, everything, False)
-        diagonal(0, out_ref, 0)
+        own_columns(0)
+        near_rows(odd)
 
         def first_rows(u):
             arrive(0, u)
             left_rows(0, u, out_ref, everything, True)
-            result_copy(u).start()
-        groups(t, 1, True, first_rows)
+
+        def first_step(u):
+            @pl.when(u != ahead)
+            def _():
+                halos_here(u)
+            group_rows(odd, u)
+
+            @pl.when(u == ahead)
+            def _():
+                left_rows(0, t, out_ref, everything, False)
+
+            @pl.when(u != ahead)
+            def _():
+                first_rows(u - s)
+                result_copy(u - s).start()
+        groups(t, 1, has_ahead, first_step)
+
+        @pl.when(has_ahead)
+        def _():
+            arrive(0, far_end)
+
+            @pl.when(jnp.logical_not(has_behind))
+            def _():
+                signal_partner()
+            left_rows(0, far_end, out_ref, everything, True)
+            wait_partner()
+            result_copy(far_end).start()
+
+        @pl.when(jnp.logical_not(has_ahead))
+        def _():
+            left_rows(0, t, out_ref, everything, False)
+        diagonal(0, out_ref, 0)
 
         @pl.when(has_behind)
         def _():
@@ -396,6 +485,7 @@
             dma((ranks,)),
             dma((ranks,)),
             dma((3,)),
+            pltpu.SemaphoreType.REGULAR,
         ],
         compiler_params=pltpu.CompilerParams(
             collective_id=0, has_side_effects=True, vmem_limit_bytes=58 * 1024 * 1024

time: 158 us -> 127 us (0.80)
  the two profiles are of different devices: /device:TPU:1 before, /device:TPU:5 now
where the time goes in v2:
time: 127 us; the launch traced here: 126 us
  Pallas kernels  123 us (97%)
  local copies, waits for them, and re-layouts  2.61 us (2%)
    pallas_call x1, Pallas kernels, per_device(): pl.pallas_call(functools.partial(kernel, parts, ranks), out_shape=(pltpu....  123 us
    unnamed x2, local copies, waits for them, and re-layouts  2.61 us

profile of v2, /device:TPU:5, one launch (start us, length us, event | category | flops | bytes accessed | tf_op | source)
XLA Modules:
  0.0 126.3 jit_solution(570439846772590544)
XLA Ops:
  0.6 123.1 %shard_map.59 = (f32[2048,512]{1,0:T(8,128)S(1)}, f32[2,512]{1,0:T(2,128)S(1)}) custom-call(bf16[2,2048,512]{2,1,0:T(8,128)(2,1)} %local_ref.1, f32[1,2048,512]{2,1,0:T(8,128)} %seed_ref.1, f32[2,12,128,128]{3,2,1,0:T(8,128)} %bitcast.4, s32[3,2,4]{2,1,0:T(2,128)} %bitcast.5), custom_call_target="tpu_custom_call" | custom-call | tf_op jit(solution)/shard_map/pallas_call | solution.py:463
  123.7 2.0 %copy.8 = f32[1,2048,512]{2,1,0:T(8,128)} copy(f32[1,2048,512]{2,1,0:T(8,128)S(1)} %bitcast.3) | data formatting | bytes 8388608
  125.7 0.6 copy.9

commit v3 on v2

--- a/solution.py
+++ b/solution.py
@@ -76,8 +76,9 @@
         nxt[...] = jnp.zeros_like(nxt)
 
     for ref in (m_high, m_low):
-        ref[pl.ds(0, tr), :] = jnp.zeros((tr, width), BF16)
-        ref[pl.ds(tr + rows, tr), :] = jnp.zeros((tr, width), BF16)
+        for j in (0, 1):
+            ref[j, pl.ds(0, tr), :] = jnp.zeros((tr, width), BF16)
+            ref[j, pl.ds(tr + rows, tr), :] = jnp.zeros((tr, width), BF16)
     for ref in (wc_high, wc_low, wt_high, wt_low):
         ref[...] = jnp.zeros_like(ref)
     for j in (1, 0):
@@ -140,34 +141,51 @@
                 send_sem=nsend.at[kind, u], recv_sem=nrecv.at[kind, u],
                 device_id={"tm": p - 1, "tile": target}, device_id_type=MESH)
 
+        def lead(u, direction):
+            return tile(u * lt if direction > 0 else (u + 1) * lt - 1)
+
+        def rest(u, direction):
+            return pl.ds(pl.multiple_of(u * width + (tr if direction > 0 else 0), tr), width - tr)
+
         def seeds(action):
             low, high = pl.ds(0, tr), pl.ds(width - tr, tr)
             toward, back = (low, high) if s > 0 else (high, low)
-            sends = p > 0
             number = t if s > 0 else ranks - 1 - t
 
-            def walk(start, does, one):
-                @pl.when(does)
+            def pieces(u, source, place, kind, target):
+                action(seed_copy((lead(u, -s), source), (lead(u, -s), place), kind + 5, u, target))
+                if lt > 1:
+                    action(seed_copy((rest(u, -s), source), (rest(u, -s), place), kind, u, target))
+
+            @pl.when(p > 0)
+            def _():
+                @pl.when(has_ahead)
                 def _():
-                    @pl.loop(start, number + 1)
-                    def _(k):
-                        one(t - s * k)
-
-            walk(0, sends & has_ahead, lambda u: action(
-                seed_copy((block(u), back), (block(u), halo_behind), 2, u, ahead)))
-            walk(2, sends & has_behind, lambda u: action(
-                seed_copy((block(u), toward), (block(u), halo_ahead), 1, u, behind)))
-
-            @pl.when(sends & has_behind)
-            def _():
-                corner = tile(t * lt if s > 0 else (t + 1) * lt - 1)
-                action(seed_copy((corner, toward), (corner, halo_ahead), 4, 0, behind))
-
-            @pl.when(sends & has_ahead)
-            def _():
-                row = tile(tile_ahead)
-                action(seed_copy((row, everything), (row, inner), 3, 0, t))
-            walk(0, sends, lambda u: action(seed_copy((block(u), everything), (block(u), inner), 0, u, t)))
+                    row = tile(tile_ahead)
+                    action(seed_copy((row, everything), (row, inner), 3, 0, t))
+
+                @pl.when(has_behind)
+                def _():
+                    corner = tile(t * lt if s > 0 else (t + 1) * lt - 1)
+                    action(seed_copy((corner, toward), (corner, halo_ahead), 4, 0, behind))
+                action(seed_copy((block(t), everything), (block(t), inner), 0, t, t))
+
+                @pl.when(has_ahead)
+                def _():
+                    pieces(t, back, halo_behind, 2, ahead)
+
+                @pl.loop(1, number + 1)
+                def _(k):
+                    u = t - s * k
+                    pieces(u, everything, inner, 0, t)
+
+                    @pl.when(has_ahead)
+                    def _():
+                        pieces(u, back, halo_behind, 2, ahead)
+
+                    @pl.when(k > 1)
+                    def _():
+                        pieces(u, toward, halo_ahead, 1, behind)
 
         def seed_arrived(dst, kind, u):
             pltpu.make_async_remote_copy(
@@ -237,29 +255,29 @@
                 for c in range(g):
                     for k in range(3):
                         high, low = split(wbuf[j, (t * lt + i * g + c) * 3 + k])
-                        at = (i, pl.ds((c + k) * tr, tr), pl.ds(c * tr, tr))
+                        at = (j, i, pl.ds((c + k) * tr, tr), pl.ds(c * tr, tr))
                         wc_high[at] = high
                         wc_low[at] = low
 
-        def some_rows(field, start, size):
+        def some_rows(field, j, start, size):
             for i in range(lt // g):
                 high, low = split(field[pl.ds(start, size), pl.ds(i * g * tr, span)])
-                value = split_dot(high, low, wc_high[i], wc_low[i])
-                at = (pl.ds(pl.multiple_of(start + tr, tr), size), pl.ds(i * g * tr, g * tr))
+                value = split_dot(high, low, wc_high[j, i], wc_low[j, i])
+                at = (j, pl.ds(pl.multiple_of(start + tr, tr), size), pl.ds(i * g * tr, g * tr))
                 high, low = split(value)
                 m_high[at] = high
                 m_low[at] = low
 
-        def group_rows(field, u):
+        def group_rows(field, j, u):
             @pl.loop(0, width // chunk)
             def _(r):
-                some_rows(field, pl.multiple_of(u * width + r * chunk, chunk), chunk)
-
-        def near_rows(field):
+                some_rows(field, j, pl.multiple_of(u * width + r * chunk, chunk), chunk)
+
+        def near_rows(field, j):
             @pl.when(has_behind)
             def _():
-                some_rows(field, pl.multiple_of(tile_behind * tr, tr), tr)
-            group_rows(field, t)
+                some_rows(field, j, pl.multiple_of(tile_behind * tr, tr), tr)
+            group_rows(field, j, t)
 
         def left_rows(j, owner, target, columns, turned):
             @pl.loop(0, lt // g)
@@ -273,7 +291,7 @@
                         wt_low[at] = low
                 start = pl.multiple_of(begin * tr, tr)
                 source = pl.ds(start, span)
-                value = split_dot(wt_high[...], wt_low[...], m_high[source, :], m_low[source, :])
+                value = split_dot(wt_high[...], wt_low[...], m_high[j, source, :], m_low[j, source, :])
                 place = pl.ds(start, g * tr)
                 value = loc[j, place, :].astype(F32) + value
                 target[place, columns] = value
@@ -303,15 +321,90 @@
         def _():
             w_copy(0, t).start()
 
-        def seeds_here(u):
+        def seeds_here(where, u, kind):
             @pl.when(has_next)
             def _():
-                seed_arrived((block(u), inner), 0, u)
-                seed_arrived((block(u), halo_ahead), 2, u)
+                seed_arrived((where, inner), kind, u)
+                seed_arrived((where, halo_ahead), kind + 2, u)
 
             @pl.when(has_next & has_behind)
             def _():
-                seed_arrived((block(u), halo_behind), 1, u)
+                seed_arrived((where, halo_behind), kind + 1, u)
+
+        def seeds_lead(u):
+            seeds_here(lead(u, s), u, 5)
+
+        def seeds_rest(u):
+            if lt > 1:
+                seeds_here(rest(u, s), u, 0)
+
+        def odd_rows(u):
+            @pl.when(u != t)
+            def _():
+                arrive(1, u)
+            left_rows(1, u, odd, inner, False)
+
+            @pl.when(has_behind)
+            def _():
+                halo_behind_copy(u).start()
+
+            @pl.when(has_ahead & (u == t))
+            def _():
+                halo_corner_copy(tile_corner).start()
+
+            @pl.when(u != t)
+            def _():
+                halo_ahead_copy(u).start()
+
+        def near_first():
+            @pl.when(has_behind)
+            def _():
+                halo_corner_copy(tile_behind).wait_recv()
+                halo_ahead_copy(t).wait_recv()
+                for i in range(lt):
+                    odd[tile(tile_behind), pl.ds(tr + i * tr, tr)] = odd[own_tile(i), halo_behind].T
+            mirror_ahead(odd)
+            near_rows(odd, 0)
+
+        def first_step(u):
+            halo_behind_copy(u).wait_recv()
+
+            @pl.when(has_behind)
+            def _():
+                halo_ahead_copy(u).wait_recv()
+
+            @pl.when(u == ahead)
+            def _():
+                near_first()
+            group_rows(odd, 0, u)
+
+            @pl.when(u == ahead)
+            def _():
+                left_rows(0, t, out_ref, everything, False)
+
+            @pl.when(u != ahead)
+            def _():
+                arrive(0, u - s)
+                left_rows(0, u - s, out_ref, everything, True)
+                result_copy(u - s).start()
+
+        def odd_step(u):
+            @pl.when(u != ahead)
+            def _():
+                seeds_lead(u)
+            some_rows(nxt, 1, pl.multiple_of(lead(u, s).start, tr), tr)
+            odd_rows(u - s)
+            if s < 0:
+                @pl.when(has_behind)
+                def _():
+                    pass_one(0, u)
+
+                @pl.when(u != ahead)
+                def _():
+                    first_step(u - s)
+            seeds_rest(u)
+            if lt > 1:
+                some_rows(nxt, 1, pl.multiple_of(rest(u, s).start, tr), width - tr)
 
         @pl.when(has_next)
         def _():
@@ -324,7 +417,7 @@
 
         @pl.when(has_ahead)
         def _():
-            seeds_here(ahead)
+            seeds_lead(ahead)
 
         @pl.when(has_behind)
         def _():
@@ -332,90 +425,20 @@
                 nxt[own_tile(i), halo_behind] = nxt[tile(tile_behind), pl.ds(tr + i * tr, tr)].T
         mirror_ahead(nxt)
         own_columns(1)
-        near_rows(nxt)
+        own_columns(0)
+        near_rows(nxt, 1)
         locals_in.wait()
-
-        def odd_rows(u):
-            @pl.when(u != t)
-            def _():
-                arrive(1, u)
-            left_rows(1, u, odd, inner, False)
-
-            @pl.when(has_behind)
-            def _():
-                halo_behind_copy(u).start()
-
-            @pl.when(has_ahead & (u == t))
-            def _():
-                halo_corner_copy(tile_corner).start()
-
-            @pl.when(u != t)
-            def _():
-                halo_ahead_copy(u).start()
-
-        def odd_step(u):
-            if s < 0:
-                @pl.when(has_behind)
-                def _():
-                    pass_one(0, u)
-
-            @pl.when(u != ahead)
-            def _():
-                seeds_here(u)
-            group_rows(nxt, u)
-            odd_rows(u - s)
         groups(t, 1, has_ahead, odd_step)
         odd_rows(far_end)
+        diagonal(1, odd, tr)
         if s > 0:
             pass_on(0)
-        diagonal(1, odd, tr)
-
-        def halos_here(u):
-            halo_behind_copy(u).wait_recv()
-
-            @pl.when(has_behind)
-            def _():
-                halo_ahead_copy(u).wait_recv()
-
-        @pl.when(has_behind)
-        def _():
-            halo_corner_copy(tile_behind).wait_recv()
-            halo_ahead_copy(t).wait_recv()
+            groups(t, 1, has_ahead, first_step)
 
         @pl.when(has_ahead)
         def _():
-            halos_here(ahead)
-
-        @pl.when(has_behind)
-        def _():
-            for i in range(lt):
-                odd[tile(tile_behind), pl.ds(tr + i * tr, tr)] = odd[own_tile(i), halo_behind].T
-        mirror_ahead(odd)
-        own_columns(0)
-        near_rows(odd)
-
-        def first_rows(u):
-            arrive(0, u)
-            left_rows(0, u, out_ref, everything, True)
-
-        def first_step(u):
-            @pl.when(u != ahead)
-            def _():
-                halos_here(u)
-            group_rows(odd, u)
-
-            @pl.when(u == ahead)
-            def _():
-                left_rows(0, t, out_ref, everything, False)
-
-            @pl.when(u != ahead)
-            def _():
-                first_rows(u - s)
-                result_copy(u - s).start()
-        groups(t, 1, has_ahead, first_step)
-
-        @pl.when(has_ahead)
-        def _():
+            if s < 0:
+                first_step(far_end)
             arrive(0, far_end)
 
             @pl.when(jnp.logical_not(has_behind))
@@ -427,6 +450,7 @@
 
         @pl.when(jnp.logical_not(has_ahead))
         def _():
+            near_first()
             left_rows(0, t, out_ref, everything, False)
         diagonal(0, out_ref, 0)
 
@@ -469,17 +493,17 @@
             pltpu.VMEM((rows, width + 2 * tr), F32),
             pltpu.VMEM((rows, width + 2 * tr), F32),
             pltpu.VMEM((2, tiles * 3, tr, tr), F32),
-            pltpu.VMEM((rows + 2 * tr, width), BF16),
-            pltpu.VMEM((rows + 2 * tr, width), BF16),
+            pltpu.VMEM((2, rows + 2 * tr, width), BF16),
+            pltpu.VMEM((2, rows + 2 * tr, width), BF16),
             pltpu.VMEM((2, rows, width), BF16),
-            pltpu.VMEM((lt // g, span, g * tr), BF16),
-            pltpu.VMEM((lt // g, span, g * tr), BF16),
+            pltpu.VMEM((2, lt // g, span, g * tr), BF16),
+            pltpu.VMEM((2, lt // g, span, g * tr), BF16),
             pltpu.VMEM((g * tr, span), BF16),
             pltpu.VMEM((g * tr, span), BF16),
             dma((2, ranks)),
             dma((2, ranks)),
-            dma((5, ranks)),
-            dma((5, ranks)),
+            dma((8, ranks)),
+            dma((8, ranks)),
             dma((3, ranks)),
             dma((3, ranks)),
             dma((ranks,)),

time: 127 us -> 136 us (1.071)
  Pallas kernels: 123 us -> 132 us
    pallas_call x1, Pallas kernels: 123 us -> 132 us  [per_device(): pl.pallas_call(functools.partial(kernel, parts, ranks), out_shape=(pltpu....]
where the time goes in v3:
time: 136 us
  Pallas kernels  132 us (97%)
  local copies, waits for them, and re-layouts  2.61 us (2%)
    pallas_call x1, Pallas kernels, per_device(): pl.pallas_call(functools.partial(kernel, parts, ranks), out_shape=(pltpu....  132 us

profile of v3, /device:TPU:5, one launch (start us, length us, event | category | flops | bytes accessed | tf_op | source)
XLA Modules:
  0.0 135.7 jit_solution(7100954249296180482)
XLA Ops:
  0.6 132.5 %shard_map.59 = (f32[2048,512]{1,0:T(8,128)S(1)}, f32[2,512]{1,0:T(2,128)S(1)}) custom-call(bf16[2,2048,512]{2,1,0:T(8,128)(2,1)} %local_ref.1, f32[1,2048,512]{2,1,0:T(8,128)} %seed_ref.1, f32[2,12,128,128]{3,2,1,0:T(8,128)} %bitcast.4, s32[3,2,4]{2,1,0:T(2,128)} %bitcast.5), custom_call_target="tpu_custom_call" | custom-call | tf_op jit(solution)/shard_map/pallas_call | solution.py:487
  133.1 2.0 %copy.8 = f32[1,2048,512]{2,1,0:T(8,128)} copy(f32[1,2048,512]{2,1,0:T(8,128)S(1)} %bitcast.3) | data formatting | bytes 8388608
  135.1 0.6 copy.9

commit v4 on v3

--- a/solution.py
+++ b/solution.py
@@ -27,7 +27,7 @@
 
 def kernel(parts, ranks, local_ref, seed_ref, band_ref, pattern_ref, out_ref, var_ref,
            nxt, odd, wbuf, m_high, m_low, loc, wc_high, wc_low, wt_high, wt_low,
-           wsend, wrecv, nsend, nrecv, hsend, hrecv, rsend, rrecv, lsem, go):
+           wsend, wrecv, nsend, nrecv, esend, erecv, hsend, hrecv, rsend, rrecv, lsem, go):
     p, t = lax.axis_index("tm"), lax.axis_index("tile")
     rows, width = seed_ref.shape[1], seed_ref.shape[2]
     tr = wbuf.shape[3]
@@ -153,7 +153,7 @@
             number = t if s > 0 else ranks - 1 - t
 
             def pieces(u, source, place, kind, target):
-                action(seed_copy((lead(u, -s), source), (lead(u, -s), place), kind + 5, u, target))
+                action(seed_copy((lead(u, -s), source), (lead(u, -s), place), kind + 1, u, target))
                 if lt > 1:
                     action(seed_copy((rest(u, -s), source), (rest(u, -s), place), kind, u, target))
 
@@ -162,35 +162,75 @@
                 @pl.when(has_ahead)
                 def _():
                     row = tile(tile_ahead)
-                    action(seed_copy((row, everything), (row, inner), 3, 0, t))
-
-                @pl.when(has_behind)
-                def _():
-                    corner = tile(t * lt if s > 0 else (t + 1) * lt - 1)
-                    action(seed_copy((corner, toward), (corner, halo_ahead), 4, 0, behind))
+                    action(seed_copy((row, everything), (row, inner), 6, 0, t))
+
+                if s < 0:
+                    @pl.when(has_behind)
+                    def _():
+                        corner = tile((t + 1) * lt - 1)
+                        action(seed_copy((corner, toward), (corner, halo_ahead), 7, 0, behind))
                 action(seed_copy((block(t), everything), (block(t), inner), 0, t, t))
 
-                @pl.when(has_ahead)
-                def _():
-                    pieces(t, back, halo_behind, 2, ahead)
+                if s < 0:
+                    @pl.when(has_ahead)
+                    def _():
+                        pieces(t, back, halo_behind, 4, ahead)
 
                 @pl.loop(1, number + 1)
                 def _(k):
                     u = t - s * k
                     pieces(u, everything, inner, 0, t)
-
-                    @pl.when(has_ahead)
-                    def _():
-                        pieces(u, back, halo_behind, 2, ahead)
-
-                    @pl.when(k > 1)
-                    def _():
-                        pieces(u, toward, halo_ahead, 1, behind)
-
-        def seed_arrived(dst, kind, u):
+                    if s < 0:
+                        @pl.when(has_ahead)
+                        def _():
+                            pieces(u, back, halo_behind, 4, ahead)
+
+                        @pl.when(k > 1)
+                        def _():
+                            pieces(u, toward, halo_ahead, 2, behind)
+
+        def seed_arrived(place, lanes, kind, u):
             pltpu.make_async_remote_copy(
-                src_ref=nxt.at[dst], dst_ref=nxt.at[dst], send_sem=nsend.at[kind, u], recv_sem=nrecv.at[kind, u],
+                src_ref=nxt.at[place, lanes], dst_ref=nxt.at[place, lanes],
+                send_sem=nsend.at[kind, u], recv_sem=nrecv.at[kind, u],
                 device_id={"tile": behind}, device_id_type=MESH).wait_recv()
+
+        def edge_copy(place, source, target_place, kind, u, target):
+            return pltpu.make_async_remote_copy(
+                src_ref=nxt.at[place, source], dst_ref=nxt.at[place, target_place],
+                send_sem=esend.at[kind, u], recv_sem=erecv.at[kind, u],
+                device_id={"tile": target}, device_id_type=MESH)
+
+        def edge_ahead_copy(place, kind, u):
+            return edge_copy(place, edge_ahead, halo_behind, kind, u, ahead)
+
+        def edge_behind_copy(place, kind, u):
+            return edge_copy(place, edge_behind, halo_ahead, kind + 2, u, behind)
+
+        def edges(place, kind, u, action):
+            @pl.when(has_behind)
+            def _():
+                action(edge_behind_copy(place, kind, u))
+
+            @pl.when((u != t) & (u != ahead))
+            def _():
+                action(edge_ahead_copy(place, kind, u))
+
+        def all_edges(action):
+            @pl.when(has_next)
+            def _():
+                @pl.loop(0, count + 1)
+                def _(k):
+                    group_edges(t + s * k, action)
+
+                @pl.when(has_ahead)
+                def _():
+                    action(edge_ahead_copy(tile(tile_corner), 4, 0))
+
+        def group_edges(u, action):
+            edges(lead(u, s), 1, u, action)
+            if lt > 1:
+                edges(rest(u, s), 0, u, action)
 
         def halo_copy(place, source, target_place, kind, u, target):
             return pltpu.make_async_remote_copy(
@@ -315,28 +355,69 @@
         seeds(lambda copy: copy.start())
         clear_halo(odd, True)
         clear_halo(nxt, has_next)
-        pass_on(1)
-
-        @pl.when(has_behind)
-        def _():
-            w_copy(0, t).start()
-
-        def seeds_here(where, u, kind):
+        own_columns(1)
+        own_columns(0)
+
+        def near_seeds():
             @pl.when(has_next)
             def _():
-                seed_arrived((where, inner), kind, u)
-                seed_arrived((where, halo_ahead), kind + 2, u)
-
-            @pl.when(has_next & has_behind)
-            def _():
-                seed_arrived((where, halo_behind), kind + 1, u)
+                seed_arrived(block(t), inner, 0, t)
+                if s < 0:
+                    group_edges(t, lambda copy: copy.start())
+
+                    @pl.when(has_ahead)
+                    def _():
+                        edge_ahead_copy(tile(tile_corner), 4, 0).start()
+
+        def column_seeds(u):
+            @pl.when(has_next)
+            def _():
+                seed_arrived(lead(u, s), inner, 1, u)
+                if lt > 1:
+                    seed_arrived(rest(u, s), inner, 0, u)
+                group_edges(u, lambda copy: copy.start())
+
+        def seeds_here(place, kind, u):
+            if s > 0:
+                @pl.when(has_next)
+                def _():
+                    seed_arrived(place, inner, kind, u)
+                    seed_arrived(place, halo_ahead, kind + 4, u)
+
+                @pl.when(has_next & has_behind)
+                def _():
+                    seed_arrived(place, halo_behind, kind + 2, u)
+            else:
+                @pl.when(has_next)
+                def _():
+                    edge_behind_copy(place, kind, u).wait_recv()
+
+                @pl.when(has_next & has_behind)
+                def _():
+                    edge_ahead_copy(place, kind, u).wait_recv()
 
         def seeds_lead(u):
-            seeds_here(lead(u, s), u, 5)
+            seeds_here(lead(u, s), 1, u)
 
         def seeds_rest(u):
             if lt > 1:
-                seeds_here(rest(u, s), u, 0)
+                seeds_here(rest(u, s), 0, u)
+
+        def near_odd():
+            @pl.when(has_next & has_behind)
+            def _():
+                seed_arrived(tile(tile_behind), inner, 6, 0)
+                if s > 0:
+                    seed_arrived(tile(tile_behind), halo_behind, 7, 0)
+                else:
+                    edge_ahead_copy(tile(tile_behind), 4, 0).wait_recv()
+
+            @pl.when(has_behind)
+            def _():
+                for i in range(lt):
+                    nxt[own_tile(i), halo_behind] = nxt[tile(tile_behind), pl.ds(tr + i * tr, tr)].T
+            mirror_ahead(nxt)
+            near_rows(nxt, 1)
 
         def odd_rows(u):
             @pl.when(u != t)
@@ -389,56 +470,70 @@
                 result_copy(u - s).start()
 
         def odd_step(u):
-            @pl.when(u != ahead)
-            def _():
-                seeds_lead(u)
+            seeds_lead(u)
+
+            @pl.when(u == ahead)
+            def _():
+                near_odd()
             some_rows(nxt, 1, pl.multiple_of(lead(u, s).start, tr), tr)
             odd_rows(u - s)
-            if s < 0:
-                @pl.when(has_behind)
-                def _():
-                    pass_one(0, u)
-
-                @pl.when(u != ahead)
-                def _():
-                    first_step(u - s)
             seeds_rest(u)
             if lt > 1:
                 some_rows(nxt, 1, pl.multiple_of(rest(u, s).start, tr), width - tr)
 
-        @pl.when(has_next)
+        locals_in.wait()
+        if s > 0:
+            pass_on(1)
+
+            @pl.when(has_behind)
+            def _():
+                w_copy(0, t).start()
+            near_seeds()
+            groups(t, 1, has_ahead, odd_step)
+        else:
+            @pl.when(has_behind & has_ahead)
+            def _():
+                pass_one(1, ahead)
+            near_seeds()
+
+            @pl.when(has_behind)
+            def _():
+                w_copy(0, t).start()
+
+            def seed_step(u):
+                @pl.when(has_behind & (u != ahead))
+                def _():
+                    pass_one(1, u)
+                column_seeds(u)
+
+                @pl.when(jnp.logical_not(has_behind))
+                def _():
+                    odd_step(u)
+            groups(t, 1, has_ahead, seed_step)
+
+            def odd_later(u):
+                @pl.when((u != far_end) | (count != ranks - 2))
+                def _():
+                    pass_one(0, u)
+            groups(t, 1, has_behind & has_ahead, odd_later)
+            groups(t, 1, has_behind & has_ahead, odd_step)
+
+        @pl.when(jnp.logical_not(has_ahead))
         def _():
-            seed_arrived((block(t), inner), 0, t)
-
-        @pl.when(has_next & has_behind)
-        def _():
-            seed_arrived((tile(tile_behind), inner), 3, 0)
-            seed_arrived((tile(tile_behind), halo_behind), 4, 0)
-
-        @pl.when(has_ahead)
-        def _():
-            seeds_lead(ahead)
-
-        @pl.when(has_behind)
-        def _():
-            for i in range(lt):
-                nxt[own_tile(i), halo_behind] = nxt[tile(tile_behind), pl.ds(tr + i * tr, tr)].T
-        mirror_ahead(nxt)
-        own_columns(1)
-        own_columns(0)
-        near_rows(nxt, 1)
-        locals_in.wait()
-        groups(t, 1, has_ahead, odd_step)
+            near_odd()
         odd_rows(far_end)
         diagonal(1, odd, tr)
         if s > 0:
             pass_on(0)
-            groups(t, 1, has_ahead, first_step)
+        else:
+            @pl.when(has_ahead & (count == ranks - 2))
+            def _():
+                pass_one(0, far_end)
+            all_edges(lambda copy: copy.wait_send())
+        groups(t, 1, has_ahead, first_step)
 
         @pl.when(has_ahead)
         def _():
-            if s < 0:
-                first_step(far_end)
             arrive(0, far_end)
 
             @pl.when(jnp.logical_not(has_behind))
@@ -504,6 +599,8 @@
             dma((2, ranks)),
             dma((8, ranks)),
             dma((8, ranks)),
+            dma((5, ranks)),
+            dma((5, ranks)),
             dma((3, ranks)),
             dma((3, ranks)),
             dma((ranks,)),

time: 136 us -> 121 us (0.89)
  Pallas kernels: 132 us -> 117 us
    pallas_call x1, Pallas kernels: 132 us -> 117 us  [per_device(): pl.pallas_call(functools.partial(kernel, parts, ranks), out_shape=(pltpu....]
where the time goes in v4:
time: 121 us; the launch traced here: 120 us
  Pallas kernels  117 us (97%)
  local copies, waits for them, and re-layouts  2.61 us (2%)
    pallas_call x1, Pallas kernels, per_device(): pl.pallas_call(functools.partial(kernel, parts, ranks), out_shape=(pltpu....  117 us
    unnamed x2, local copies, waits for them, and re-layouts  2.61 us

profile of v4, /device:TPU:5, one launch (start us, length us, event | category | flops | bytes accessed | tf_op | source)
XLA Modules:
  0.0 120.3 jit_solution(7854442417961840933)
XLA Ops:
  0.6 117.1 %shard_map.59 = (f32[2048,512]{1,0:T(8,128)S(1)}, f32[2,512]{1,0:T(2,128)S(1)}) custom-call(bf16[2,2048,512]{2,1,0:T(8,128)(2,1)} %local_ref.1, f32[1,2048,512]{2,1,0:T(8,128)} %seed_ref.1, f32[2,12,128,128]{3,2,1,0:T(8,128)} %bitcast.4, s32[3,2,4]{2,1,0:T(2,128)} %bitcast.5), custom_call_target="tpu_custom_call" | custom-call | tf_op jit(solution)/shard_map/pallas_call | solution.py:582
  117.7 2.0 %copy.8 = f32[1,2048,512]{2,1,0:T(8,128)} copy(f32[1,2048,512]{2,1,0:T(8,128)S(1)} %bitcast.3) | data formatting | bytes 8388608
  119.7 0.6 copy.9

commit v5 on v4

--- a/solution.py
+++ b/solution.py
@@ -81,6 +81,14 @@
             ref[j, pl.ds(tr + rows, tr), :] = jnp.zeros((tr, width), BF16)
     for ref in (wc_high, wc_low, wt_high, wt_low):
         ref[...] = jnp.zeros_like(ref)
+    for j in (0, 1):
+        @pl.when(t > 0)
+        def _(j=j):
+            wbuf[j, 0] = jnp.zeros((tr, tr), F32)
+
+        @pl.when(t < ranks - 1)
+        def _(j=j):
+            wbuf[j, wbuf.shape[1] - 1] = jnp.zeros((tr, tr), F32)
     for j in (1, 0):
         own_local[j].wait()
         for b in range(lt):
@@ -104,6 +112,7 @@
         edge_behind, edge_ahead = (first, last) if s > 0 else (last, first)
         halo_behind, halo_ahead = (left, right) if s > 0 else (right, left)
         tile_behind, tile_ahead = (t * lt - 1, (t + 1) * lt) if s > 0 else ((t + 1) * lt, t * lt - 1)
+        end = ranks - 1 if s > 0 else 0
         tile_corner = (t + 1) * lt - 1 if s > 0 else t * lt
 
         def groups(base, start, does, action):
@@ -116,15 +125,24 @@
                     action(base + s * k)
 
 
-        def w_copy(j, u):
-            part = wbuf.at[j, pl.ds(u * lt * 3, lt * 3)]
-            return pltpu.make_async_remote_copy(
-                src_ref=part, dst_ref=part, send_sem=wsend.at[j, u], recv_sem=wrecv.at[j, u],
-                device_id={"tile": behind}, device_id_type=MESH)
+        def w_copy(j, u, action):
+            for condition, skip in ((u == end, 1), (u != end, 0)):
+                @pl.when(condition)
+                def _(skip=skip):
+                    part = wbuf.at[j, pl.ds(u * lt * 3 + (skip if s < 0 else 0), lt * 3 - skip)]
+                    action(pltpu.make_async_remote_copy(
+                        src_ref=part, dst_ref=part, send_sem=wsend.at[j, u], recv_sem=wrecv.at[j, u],
+                        device_id={"tile": behind}, device_id_type=MESH))
+
+        def w_start(j, u):
+            w_copy(j, u, lambda copy: copy.start())
+
+        def w_here(j, u):
+            w_copy(j, u, lambda copy: copy.wait_recv())
 
         def pass_one(j, u):
-            w_copy(j, u).wait_recv()
-            w_copy(j, u).start()
+            w_here(j, u)
+            w_start(j, u)
 
         def pass_on(j):
             groups(t, 1, has_behind, lambda u: pass_one(j, u))
@@ -132,7 +150,7 @@
         def arrive(j, u):
             @pl.when(jnp.logical_not(has_behind))
             def _():
-                w_copy(j, u).wait_recv()
+                w_here(j, u)
 
 
         def seed_copy(src, dst, kind, u, target):
@@ -141,6 +159,9 @@
                 send_sem=nsend.at[kind, u], recv_sem=nrecv.at[kind, u],
                 device_id={"tm": p - 1, "tile": target}, device_id_type=MESH)
 
+        def own_strip(c):
+            return pl.ds(pl.multiple_of(t * width + c * tr, tr), width - c * tr)
+
         def lead(u, direction):
             return tile(u * lt if direction > 0 else (u + 1) * lt - 1)
 
@@ -169,7 +190,9 @@
                     def _():
                         corner = tile((t + 1) * lt - 1)
                         action(seed_copy((corner, toward), (corner, halo_ahead), 7, 0, behind))
-                action(seed_copy((block(t), everything), (block(t), inner), 0, t, t))
+                for c in range(lt):
+                    strip = own_strip(c)
+                    action(seed_copy((strip, pl.ds(c * tr, tr)), (strip, pl.ds(tr + c * tr, tr)), 8, c, t))
 
                 if s < 0:
                     @pl.when(has_ahead)
@@ -351,7 +374,7 @@
 
         @pl.when(has_behind)
         def _():
-            w_copy(1, t).start()
+            w_start(1, t)
         seeds(lambda copy: copy.start())
         clear_halo(odd, True)
         clear_halo(nxt, has_next)
@@ -361,7 +384,11 @@
         def near_seeds():
             @pl.when(has_next)
             def _():
-                seed_arrived(block(t), inner, 0, t)
+                for c in range(lt):
+                    seed_arrived(own_strip(c), pl.ds(tr + c * tr, tr), 8, c)
+                for c in range(lt):
+                    for r in range(c + 1, lt):
+                        nxt[own_tile(c), pl.ds(tr + r * tr, tr)] = nxt[own_tile(r), pl.ds(tr + c * tr, tr)].T
                 if s < 0:
                     group_edges(t, lambda copy: copy.start())
 
@@ -459,10 +486,6 @@
                 near_first()
             group_rows(odd, 0, u)
 
-            @pl.when(u == ahead)
-            def _():
-                left_rows(0, t, out_ref, everything, False)
-
             @pl.when(u != ahead)
             def _():
                 arrive(0, u - s)
@@ -487,7 +510,7 @@
 
             @pl.when(has_behind)
             def _():
-                w_copy(0, t).start()
+                w_start(0, t)
             near_seeds()
             groups(t, 1, has_ahead, odd_step)
         else:
@@ -498,7 +521,7 @@
 
             @pl.when(has_behind)
             def _():
-                w_copy(0, t).start()
+                w_start(0, t)
 
             def seed_step(u):
                 @pl.when(has_behind & (u != ahead))
@@ -534,11 +557,10 @@
 
         @pl.when(has_ahead)
         def _():
+            @pl.when(jnp.logical_not(has_behind))
+            def _():
+                signal_partner()
             arrive(0, far_end)
-
-            @pl.when(jnp.logical_not(has_behind))
-            def _():
-                signal_partner()
             left_rows(0, far_end, out_ref, everything, True)
             wait_partner()
             result_copy(far_end).start()
@@ -546,7 +568,7 @@
         @pl.when(jnp.logical_not(has_ahead))
         def _():
             near_first()
-            left_rows(0, t, out_ref, everything, False)
+        left_rows(0, t, out_ref, everything, False)
         diagonal(0, out_ref, 0)
 
         @pl.when(has_behind)
@@ -556,7 +578,7 @@
                 result_arrived(t - s * k)
 
         for j in (1, 0):
-            groups(t, 0, has_behind, lambda u, j=j: w_copy(j, u).wait_send())
+            groups(t, 0, has_behind, lambda u, j=j: w_copy(j, u, lambda copy: copy.wait_send()))
         seeds(lambda copy: copy.wait_send())
         groups(t, 0, has_behind, lambda u: halo_behind_copy(u).wait_send())
 
@@ -597,8 +619,8 @@
             pltpu.VMEM((g * tr, span), BF16),
             dma((2, ranks)),
             dma((2, ranks)),
-            dma((8, ranks)),
-            dma((8, ranks)),
+            dma((9, max(ranks, lt))),
+            dma((9, max(ranks, lt))),
             dma((5, ranks)),
             dma((5, ranks)),
             dma((3, ranks)),

time: 121 us -> 116 us (0.959)
  Pallas kernels: 117 us -> 112 us
    pallas_call x1, Pallas kernels: 117 us -> 112 us  [per_device(): pl.pallas_call(functools.partial(kernel, parts, ranks), out_shape=(pltpu....]
where the time goes in v5:
time: 116 us; the launch traced here: 115 us
  Pallas kernels  112 us (97%)
  local copies, waits for them, and re-layouts  2.61 us (2%)
    pallas_call x1, Pallas kernels, per_device(): pl.pallas_call(functools.partial(kernel, parts, ranks), out_shape=(pltpu....  112 us
    unnamed x2, local copies, waits for them, and re-layouts  2.61 us

profile of v5, /device:TPU:5, one launch (start us, length us, event | category | flops | bytes accessed | tf_op | source)
XLA Modules:
  0.0 115.1 jit_solution(13495872609022077373)
XLA Ops:
  0.6 111.8 %shard_map.59 = (f32[2048,512]{1,0:T(8,128)S(1)}, f32[2,512]{1,0:T(2,128)S(1)}) custom-call(bf16[2,2048,512]{2,1,0:T(8,128)(2,1)} %local_ref.1, f32[1,2048,512]{2,1,0:T(8,128)} %seed_ref.1, f32[2,12,128,128]{3,2,1,0:T(8,128)} %bitcast.4, s32[3,2,4]{2,1,0:T(2,128)} %bitcast.5), custom_call_target="tpu_custom_call" | custom-call | tf_op jit(solution)/shard_map/pallas_call | solution.py:604
  112.5 2.0 %copy.8 = f32[1,2048,512]{2,1,0:T(8,128)} copy(f32[1,2048,512]{2,1,0:T(8,128)S(1)} %bitcast.3) | data formatting | bytes 8388608
  114.5 0.6 copy.9

commit v6 on v5

--- a/solution.py
+++ b/solution.py
@@ -27,7 +27,7 @@
 
 def kernel(parts, ranks, local_ref, seed_ref, band_ref, pattern_ref, out_ref, var_ref,
            nxt, odd, wbuf, m_high, m_low, loc, wc_high, wc_low, wt_high, wt_low,
-           wsend, wrecv, nsend, nrecv, esend, erecv, hsend, hrecv, rsend, rrecv, lsem, go):
+           wsend, wrecv, nsend, nrecv, esend, hsend, hrecv, rsend, rrecv, lsem, go):
     p, t = lax.axis_index("tm"), lax.axis_index("tile")
     rows, width = seed_ref.shape[1], seed_ref.shape[2]
     tr = wbuf.shape[3]
@@ -55,15 +55,16 @@
         if paired:
             greet(partner, u)
 
+    reach = (0,) if paired else (-1, 0, 1)
     for a in (-1, 1):
-        for b in (-1, 0, 1):
+        for b in reach:
             meet = (p + a >= 0) & (p + a < parts) & (t + b >= 0) & (t + b < ranks)
 
             @pl.when(meet & (p + a != partner) if paired else meet)
             def _(a=a, b=b):
                 greet(p + a, t + b)
     near_tm = jnp.where(p > 0, 1, 0) + jnp.where(p < parts - 1, 1, 0) - (1 if paired else 0)
-    near_tile = 1 + jnp.where(t > 0, 1, 0) + jnp.where(t < ranks - 1, 1, 0)
+    near_tile = 1 if paired else 1 + jnp.where(t > 0, 1, 0) + jnp.where(t < ranks - 1, 1, 0)
     meets = ranks - 1 + (ranks if paired else 0) + near_tm * near_tile
     own_local = [pltpu.make_async_copy(band_ref.at[j], wbuf.at[j, pl.ds(t * lt * 3, lt * 3)], lsem.at[j]) for j in (0, 1)]
     locals_in = pltpu.make_async_copy(local_ref, loc, lsem.at[2])
@@ -183,16 +184,16 @@
                 @pl.when(has_ahead)
                 def _():
                     row = tile(tile_ahead)
-                    action(seed_copy((row, everything), (row, inner), 6, 0, t))
+                    action(seed_copy((row, everything), (row, inner), 0, t, t))
 
                 if s < 0:
                     @pl.when(has_behind)
                     def _():
                         corner = tile((t + 1) * lt - 1)
-                        action(seed_copy((corner, toward), (corner, halo_ahead), 7, 0, behind))
+                        action(seed_copy((corner, toward), (corner, halo_ahead), 2, behind, behind))
                 for c in range(lt):
                     strip = own_strip(c)
-                    action(seed_copy((strip, pl.ds(c * tr, tr)), (strip, pl.ds(tr + c * tr, tr)), 8, c, t))
+                    action(seed_copy((strip, pl.ds(c * tr, tr)), (strip, pl.ds(tr + c * tr, tr)), 6, c, t))
 
                 if s < 0:
                     @pl.when(has_ahead)
@@ -218,17 +219,20 @@
                 send_sem=nsend.at[kind, u], recv_sem=nrecv.at[kind, u],
                 device_id={"tile": behind}, device_id_type=MESH).wait_recv()
 
-        def edge_copy(place, source, target_place, kind, u, target):
+        def edge_copy(place, source, target_place, sent, landed, u, target):
             return pltpu.make_async_remote_copy(
                 src_ref=nxt.at[place, source], dst_ref=nxt.at[place, target_place],
-                send_sem=esend.at[kind, u], recv_sem=erecv.at[kind, u],
+                send_sem=esend.at[sent], recv_sem=nrecv.at[landed, u],
                 device_id={"tile": target}, device_id_type=MESH)
 
         def edge_ahead_copy(place, kind, u):
-            return edge_copy(place, edge_ahead, halo_behind, kind, u, ahead)
+            return edge_copy(place, edge_ahead, halo_behind, (kind, u), kind + 2, u, ahead)
 
         def edge_behind_copy(place, kind, u):
-            return edge_copy(place, edge_behind, halo_ahead, kind + 2, u, behind)
+            return edge_copy(place, edge_behind, halo_ahead, (kind + 2, u), kind + 4, u, behind)
+
+        def edge_corner_copy(b, target):
+            return edge_copy(tile(b), edge_ahead, halo_behind, (0, t), 2, target, ahead)
 
         def edges(place, kind, u, action):
             @pl.when(has_behind)
@@ -248,7 +252,7 @@
 
                 @pl.when(has_ahead)
                 def _():
-                    action(edge_ahead_copy(tile(tile_corner), 4, 0))
+                    action(edge_corner_copy(tile_corner, ahead))
 
         def group_edges(u, action):
             edges(lead(u, s), 1, u, action)
@@ -264,8 +268,8 @@
         def halo_ahead_copy(u):
             return halo_copy(block(u), edge_ahead, halo_behind, 0, u, ahead)
 
-        def halo_corner_copy(b):
-            return halo_copy(tile(b), edge_ahead, halo_behind, 2, 0, ahead)
+        def halo_corner_copy(b, source):
+            return halo_copy(tile(b), edge_ahead, halo_behind, 0, source, ahead)
 
         def halo_behind_copy(u):
             return halo_copy(block(u), edge_behind, halo_ahead, 1, u, behind)
@@ -385,7 +389,7 @@
             @pl.when(has_next)
             def _():
                 for c in range(lt):
-                    seed_arrived(own_strip(c), pl.ds(tr + c * tr, tr), 8, c)
+                    seed_arrived(own_strip(c), pl.ds(tr + c * tr, tr), 6, c)
                 for c in range(lt):
                     for r in range(c + 1, lt):
                         nxt[own_tile(c), pl.ds(tr + r * tr, tr)] = nxt[own_tile(r), pl.ds(tr + c * tr, tr)].T
@@ -394,7 +398,7 @@
 
                     @pl.when(has_ahead)
                     def _():
-                        edge_ahead_copy(tile(tile_corner), 4, 0).start()
+                        edge_corner_copy(tile_corner, ahead).start()
 
         def column_seeds(u):
             @pl.when(has_next)
@@ -433,11 +437,11 @@
         def near_odd():
             @pl.when(has_next & has_behind)
             def _():
-                seed_arrived(tile(tile_behind), inner, 6, 0)
+                seed_arrived(tile(tile_behind), inner, 0, t)
                 if s > 0:
-                    seed_arrived(tile(tile_behind), halo_behind, 7, 0)
+                    seed_arrived(tile(tile_behind), halo_behind, 2, t)
                 else:
-                    edge_ahead_copy(tile(tile_behind), 4, 0).wait_recv()
+                    edge_corner_copy(tile_behind, t).wait_recv()
 
             @pl.when(has_behind)
             def _():
@@ -458,7 +462,7 @@
 
             @pl.when(has_ahead & (u == t))
             def _():
-                halo_corner_copy(tile_corner).start()
+                halo_corner_copy(tile_corner, t).start()
 
             @pl.when(u != t)
             def _():
@@ -467,7 +471,7 @@
         def near_first():
             @pl.when(has_behind)
             def _():
-                halo_corner_copy(tile_behind).wait_recv()
+                halo_corner_copy(tile_behind, behind).wait_recv()
                 halo_ahead_copy(t).wait_recv()
                 for i in range(lt):
                     odd[tile(tile_behind), pl.ds(tr + i * tr, tr)] = odd[own_tile(i), halo_behind].T
@@ -571,22 +575,22 @@
         left_rows(0, t, out_ref, everything, False)
         diagonal(0, out_ref, 0)
 
+        for j in (1, 0):
+            groups(t, 0, has_behind, lambda u, j=j: w_copy(j, u, lambda copy: copy.wait_send()))
+        seeds(lambda copy: copy.wait_send())
+        groups(t, 0, has_behind, lambda u: halo_behind_copy(u).wait_send())
+
+        @pl.when(has_ahead)
+        def _():
+            halo_corner_copy(tile_corner, t).wait_send()
+        groups(t, 1, has_ahead, lambda u: halo_ahead_copy(u).wait_send())
+        groups(t, 1, True, lambda u: result_copy(u).wait_send())
+
         @pl.when(has_behind)
         def _():
             @pl.loop(1, ranks - count)
             def _(k):
                 result_arrived(t - s * k)
-
-        for j in (1, 0):
-            groups(t, 0, has_behind, lambda u, j=j: w_copy(j, u, lambda copy: copy.wait_send()))
-        seeds(lambda copy: copy.wait_send())
-        groups(t, 0, has_behind, lambda u: halo_behind_copy(u).wait_send())
-
-        @pl.when(has_ahead)
-        def _():
-            halo_corner_copy(tile_corner).wait_send()
-        groups(t, 1, has_ahead, lambda u: halo_ahead_copy(u).wait_send())
-        groups(t, 1, True, lambda u: result_copy(u).wait_send())
 
     for remainder, s in ((0, 1), (1, -1)):
         @pl.when(lax.rem(p, 2) == remainder)
@@ -619,12 +623,11 @@
             pltpu.VMEM((g * tr, span), BF16),
             dma((2, ranks)),
             dma((2, ranks)),
-            dma((9, max(ranks, lt))),
-            dma((9, max(ranks, lt))),
-            dma((5, ranks)),
-            dma((5, ranks)),
-            dma((3, ranks)),
-            dma((3, ranks)),
+            dma((7, max(ranks, lt))),
+            dma((7, max(ranks, lt))),
+            dma((4, ranks)),
+            dma((2, ranks)),
+            dma((2, ranks)),
             dma((ranks,)),
             dma((ranks,)),
             dma((3,)),

time: 116 us -> 115 us (level)
  no operation moved by 1% of the time
where the time goes in v6:
time: 115 us; the launch traced here: 114 us
  Pallas kernels  111 us (97%)
  local copies, waits for them, and re-layouts  2.61 us (2%)
    pallas_call x1, Pallas kernels, per_device(): pl.pallas_call(functools.partial(kernel, parts, ranks), out_shape=(pltpu....  111 us
    unnamed x2, local copies, waits for them, and re-layouts  2.61 us

profile of v6, /device:TPU:5, one launch (start us, length us, event | category | flops | bytes accessed | tf_op | source)
XLA Modules:
  0.0 114.3 jit_solution(16192946639294673812)
XLA Ops:
  0.6 111.1 %shard_map.59 = (f32[2048,512]{1,0:T(8,128)S(1)}, f32[2,512]{1,0:T(2,128)S(1)}) custom-call(bf16[2,2048,512]{2,1,0:T(8,128)(2,1)} %local_ref.1, f32[1,2048,512]{2,1,0:T(8,128)} %seed_ref.1, f32[2,12,128,128]{3,2,1,0:T(8,128)} %bitcast.4, s32[3,2,4]{2,1,0:T(2,128)} %bitcast.5), custom_call_target="tpu_custom_call" | custom-call | tf_op jit(solution)/shard_map/pallas_call | solution.py:608
  111.7 2.0 %copy.8 = f32[1,2048,512]{2,1,0:T(8,128)} copy(f32[1,2048,512]{2,1,0:T(8,128)S(1)} %bitcast.3) | data formatting | bytes 8388608
  113.7 0.6 copy.9
